TPU v7x, 32 devices: a whole 2x2x4 slice. The times are simulated.
32 devices in a mesh: gx: 4 (over y, x), gy: 8 (over z, core).
Axes of the slice: x: 2, y: 2, z: 4, core: 2. Of those that a mesh axis runs over, the one named last changes fastest.
Arguments:
- links: float32 [4, 3, 3, 2, 8, 16, 6, 128], P(None, None, None, None, 'gx', 'gy'), may hold values from -1 to 1, as said below
- incoming: float32 [4, 3, 3, 2, 8, 16, 4, 128], P(None, None, None, None, 'gx', 'gy'), may hold values from -6 to 6
Outputs:
- force: float32 [4, 3, 3, 2, 8, 16, 4, 128], P(None, None, None, None, 'gx', 'gy')
Inputs may be any that keep to these rules, and one draw needn't show every extreme that they name: `links`: each link is a special unitary 3 x 3 matrix.
All inputs are finite; a program needn't handle non-finite values.
Results may differ from a plain program's by a relative error of at most 0.0003.
Values sent between devices are 32-bit elements; how exact they have to be, the bound alone decides.
A program may use at most 128 MiB of HBM per device.

v0:
```python
from functools import partial

import jax
import jax.numpy as jnp
from jax import lax
from jax.experimental import pallas as pl
from jax.experimental.pallas import tpu as pltpu
from jax.sharding import PartitionSpec as P

smear_weight = 0.2
MESH = pl.DeviceIdType.MESH
AXX, AXY, AXZ, AXT = 0, 1, 2, 3
SENT = 12
COMP = 18
ALG = 8
YSLOT = (1, 0, 2, 3)


def re(i, j):
    return (i * 3 + j) * 2


def cmul(a, b):
    return (a[0] * b[0] - a[1] * b[1], a[0] * b[1] + a[1] * b[0])


def cadd(a, b):
    return (a[0] + b[0], a[1] + b[1])


def conj(a):
    return (a[0], -a[1])


def row_times(row, mat, adj=False, acc=None):
    out = []
    for k in range(3):
        total_r = None if acc is None else acc[k][0]
        total_i = None if acc is None else acc[k][1]
        for j in range(3):
            b = mat(k, j) if adj else mat(j, k)
            a = row[j]
            if adj:
                r = a[0] * b[0] + a[1] * b[1]
                i = a[1] * b[0] - a[0] * b[1]
            else:
                r = a[0] * b[0] - a[1] * b[1]
                i = a[0] * b[1] + a[1] * b[0]
            total_r = r if total_r is None else total_r + r
            total_i = i if total_i is None else total_i + i
        out.append((total_r, total_i))
    return out


def getter(load):
    return lambda i, j: (load(re(i, j)), load(re(i, j) + 1))


def row_of(mat, i):
    return [mat(i, j) for j in range(3)]


def adj_row(mat, i):
    return [conj(mat(j, i)) for j in range(3)]


def full(mat):
    values = [[mat(i, j) for j in range(3)] for i in range(3)]
    return lambda i, j: values[i][j]


def of_rows(rows):
    return lambda i, j: rows[i][j]


def traceless_anti(mat):
    diag = [mat(i, i)[1] for i in range(3)]
    third = (diag[0] + diag[1] + diag[2]) * (1.0 / 3.0)
    diag = [v - third for v in diag]
    zero = jnp.zeros_like(third)
    rows = [[None] * 3 for _ in range(3)]
    for i in range(3):
        rows[i][i] = (zero, diag[i])
        for j in range(i + 1, 3):
            a, b = mat(i, j), mat(j, i)
            up = (0.5 * (a[0] - b[0]), 0.5 * (a[1] + b[1]))
            rows[i][j] = up
            rows[j][i] = (-up[0], up[1])
    return of_rows(rows)


def alg_values(mat):
    out = [mat(0, 0)[1], mat(1, 1)[1]]
    for i, j in ((0, 1), (0, 2), (1, 2)):
        out += list(mat(i, j))
    return out


def alg_matrix(load):
    v = [load(k) for k in range(ALG)]
    zero = jnp.zeros_like(v[0])
    rows = [[None] * 3 for _ in range(3)]
    rows[0][0], rows[1][1], rows[2][2] = (zero, v[0]), (zero, v[1]), (zero, -(v[0] + v[1]))
    for k, (i, j) in enumerate(((0, 1), (0, 2), (1, 2))):
        up = (v[2 + 2 * k], v[3 + 2 * k])
        rows[i][j] = up
        rows[j][i] = (-up[0], up[1])
    return of_rows(rows)


def third_row(load, store):
    g = getter(load)
    a, b = row_of(g, 0), row_of(g, 1)
    for k in range(3):
        p, q = (k + 1) % 3, (k + 2) % 3
        u, v = cmul(a[p], b[q]), cmul(a[q], b[p])
        store(re(2, k), u[0] - v[0])
        store(re(2, k) + 1, v[1] - u[1])


def kernel(
    sizes, links, inc, out,
    own, plus, minus, diag, gown, gplus, gminus, gdiag,
    sig, cst, lam,
    hxm, hxp, hym, hyp, cxy, cyx,
    cxs, cys, lcxs, lcys, bx5s, bx0s, by5s, by0s, bx5, bx0, by5, by0,
    yup, ydn, lyup, lydn,
    lxm, lxp, lym, lyp, lcxy, lcyx,
    gxm, gxp, gym, gyp, gcxy, gcyx,
    send_sem, recv_sem,
):
    nx, ny = sizes
    wx, wy = links.shape[2], links.shape[3]
    ts = links.shape[4] - 2
    rows, lanes = wy * ts, links.shape[5]
    mx, my = lax.axis_index("gx"), lax.axis_index("gy")
    xu, xd = lax.rem(mx + 1, nx), lax.rem(mx + nx - 1, nx)
    yu, yd = lax.rem(my + 1, ny), lax.rem(my + ny - 1, ny)
    peers = ((xu, my), (xd, my), (mx, yu), (mx, yd), (xu, yd), (xd, yu))

    barrier = pltpu.get_barrier_semaphore()
    for peer in peers:
        pl.semaphore_signal(barrier, inc=1, device_id=peer, device_id_type=MESH)

    row_id = lax.broadcasted_iota(jnp.int32, (rows, lanes), 0)
    t_id = lax.rem(row_id, ts)

    def sub(v, shift):
        shift = shift % rows
        return v if shift == 0 else pltpu.roll(v, shift, 0)

    def lane(v, shift):
        return pltpu.roll(v, shift % lanes, 1)

    def tiled(v):
        return jnp.concatenate([v] * wy, axis=0)

    def compact(c, _):
        for d in range(4):
            for x in range(wx):
                for y in range(wy):
                    own[d, c, x, y * ts:(y + 1) * ts, :] = links[d, c, x, y, 1:1 + ts, :]
        return 0

    def pack(c, _):
        for d in range(4):
            for x in range(wx):
                yup[YSLOT[d], c, x * ts:(x + 1) * ts, :] = links[d, c, x, wy - 1, 1:1 + ts, :]
                ydn[YSLOT[d], c, x * ts:(x + 1) * ts, :] = links[d, c, x, 0, 1:1 + ts, :]
        cxs[c] = links[AXX, c, wx - 1, 0, 1:1 + ts, :]
        cys[c] = links[AXY, c, 0, wy - 1, 1:1 + ts, :]
        for y in range(wy):
            bx5s[c, y:y + 1, :] = links[AXX, c, wx - 1, y, ts + 1:ts + 2, :]
            bx0s[c, y:y + 1, :] = links[AXT, c, 0, y, 0:1, :]
        for x in range(wx):
            by5s[c, x:x + 1, :] = links[AXY, c, x, wy - 1, ts + 1:ts + 2, :]
            by0s[c, x:x + 1, :] = links[AXT, c, x, 0, 0:1, :]
        return 0

    lax.fori_loop(0, COMP, compact, 0)
    lax.fori_loop(0, SENT, pack, 0)
    pl.semaphore_wait(barrier, len(peers))

    def exchange(items, base):
        copies = []
        for k, (src, dst, peer) in enumerate(items):
            copy = pltpu.make_async_remote_copy(
                src_ref=src, dst_ref=dst, send_sem=send_sem.at[base + k],
                recv_sem=recv_sem.at[base + k], device_id=peer, device_id_type=MESH)
            copy.start()
            copies.append(copy)
        return copies

    s = pl.ds(0, SENT)
    first = exchange((
        (own.at[:, s, wx - 1], hxm.at[:, s], peers[0]),
        (own.at[1:4, s, 0], hxp.at[1:4, s], peers[1]),
        (yup, hym.at[:, s], peers[2]),
        (ydn.at[1:4], hyp.at[1:4, s], peers[3]),
        (cxs, cxy.at[s], peers[4]),
        (cys, cyx.at[s], peers[5]),
        (bx5s, bx5.at[s], peers[0]),
        (bx0s, bx0.at[s], peers[1]),
        (by5s, by5.at[s], peers[2]),
        (by0s, by0.at[s], peers[3]),
    ), 0)

    def compact_in(c, _):
        for d in range(4):
            for x in range(wx):
                for y in range(wy):
                    sig[d, c, x, y * ts:(y + 1) * ts, :] = inc[d, c, x, y]
                cst[d, c, x] = jnp.zeros((rows, lanes), jnp.float32)
        return 0

    lax.fori_loop(0, COMP, compact_in, 0)
    def fix(ref, *index):
        def store(c, v):
            ref[(*index, c)] = v
        third_row(lambda c: ref[(*index, c)], store)

    def fix_y():
        def four(d, _):
            fix(hym, d)
            return 0

        def three(d, _):
            fix(hyp, d)
            return 0

        lax.fori_loop(0, 4, four, 0)
        lax.fori_loop(1, 4, three, 0)
        for ref in (by5, by0):
            fix(ref)

    def fix_x():
        def four(d, _):
            fix(hxm, d)
            return 0

        def three(d, _):
            fix(hxp, d)
            return 0

        lax.fori_loop(0, 4, four, 0)
        lax.fori_loop(1, 4, three, 0)
        for ref in (cxy, cyx, bx5, bx0):
            fix(ref)

    def spread(parts):
        v = jnp.broadcast_to(parts[-1], (rows, lanes))
        for y in range(wy - 2, -1, -1):
            v = jnp.where(row_id < (y + 1) * ts, jnp.broadcast_to(parts[y], (rows, lanes)), v)
        return v

    def t_ahead(v, parts):
        edge = 0.0 if parts is None else spread(parts)
        return jnp.where(t_id == ts - 1, edge, sub(v, -1))

    def t_behind(v, parts):
        edge = 0.0 if parts is None else spread(parts)
        return jnp.where(t_id == 0, edge, sub(v, 1))

    def y_ahead(v, halo, x):
        return jnp.where(row_id >= (wy - 1) * ts, sub(halo, (wy - 1 - x) * ts), sub(v, -ts))

    def y_behind(v, halo, x):
        return jnp.where(row_id < ts, sub(halo, -x * ts), sub(v, ts))

    def build(own, plus, minus, diag, hxm, hxp, hym, hyp, cxy, cyx, edges, stage):
        def low(d, c, x):
            return [links[d, c, x, y, 0:1, :] for y in range(wy)] if edges else None

        def high(d, c, x):
            return [links[d, c, x, y, ts + 1:ts + 2, :] for y in range(wy)] if edges else None

        def pick(ref, c, n):
            return [ref[c, k:k + 1, :] for k in range(n)] if edges else None

        def body(c, _):
            for x in range(wx):
                for d in range(4):
                    here = own[d, c, x]
                    if stage == 0:
                        if d != AXX:
                            plus[d, AXX, c, x] = own[d, c, x + 1] if x + 1 < wx else hxp[d, c]
                        minus[d, AXX, c, x] = own[d, c, x - 1] if x > 0 else hxm[d, c]
                    if stage == 1:
                        if d != AXY:
                            plus[d, AXY, c, x] = y_ahead(here, hyp[YSLOT[d], c], x)
                        minus[d, AXY, c, x] = y_behind(here, hym[YSLOT[d], c], x)
                    if stage == 2:
                        if d != AXZ:
                            plus[d, AXZ, c, x] = lane(here, -1)
                        if d != AXT:
                            plus[d, AXT, c, x] = t_ahead(here, high(d, c, x))
                        minus[d, AXZ, c, x] = lane(here, 1)
                        minus[d, AXT, c, x] = t_behind(here, low(d, c, x))
            for x in range(wx):
                last = x + 1 == wx
                if stage == 2:
                    diag[AXZ, AXT, c, x] = lane(plus[AXZ, AXT, c, x], 1)
                    diag[AXT, AXZ, c, x] = lane(minus[AXT, AXT, c, x], -1)
                if stage == 1:
                    back = minus[AXY, AXY, c, x]
                    diag[AXY, AXZ, c, x] = lane(back, -1)
                    parts = None
                    if edges:
                        parts = [by5[c, x:x + 1, :]] + high(AXY, c, x)[:wy - 1]
                    diag[AXY, AXT, c, x] = t_ahead(back, parts)
                    diag[AXZ, AXY, c, x] = lane(plus[AXZ, AXY, c, x], 1)
                    parts = None
                    if edges:
                        parts = low(AXT, c, x)[1:] + [by0[c, x:x + 1, :]]
                    diag[AXT, AXY, c, x] = t_behind(plus[AXT, AXY, c, x], parts)
                if stage == 0:
                    if x == 0:
                        edge = hxm[AXX, c]
                        diag[AXX, AXY, c, x] = jnp.where(
                            row_id >= (wy - 1) * ts, tiled(cxy[c]), sub(edge, -ts))
                        diag[AXX, AXZ, c, x] = lane(edge, -1)
                        diag[AXX, AXT, c, x] = t_ahead(edge, pick(bx5, c, wy))
                    else:
                        for m in (AXY, AXZ, AXT):
                            diag[AXX, m, c, x] = plus[AXX, m, c, x - 1]
                    if last:
                        diag[AXY, AXX, c, x] = jnp.where(
                            row_id < ts, tiled(cyx[c]), sub(hxp[AXY, c], ts))
                        diag[AXZ, AXX, c, x] = lane(hxp[AXZ, c], 1)
                        diag[AXT, AXX, c, x] = t_behind(hxp[AXT, c], pick(bx0, c, wy))
                    else:
                        for m in (AXY, AXZ, AXT):
                            diag[m, AXX, c, x] = minus[m, m, c, x + 1]
            return 0

        lax.fori_loop(0, COMP, body, 0)

    def build_links(stage):
        build(own, plus, minus, diag, hxm, hxp, hym, hyp, cxy, cyx, True, stage)

    def link(ref, *index):
        return getter(lambda c: ref[(*index[:-1], c, index[-1])])

    def planes(base, work):
        def step(q, _):
            pair, x = q // wx, lax.rem(q, wx)
            gap, swap = 1 + pair // 2, lax.rem(pair, 2)
            work(base + gap * swap, base + gap * (1 - swap), x)
            return 0

        lax.fori_loop(0, 2 * (3 - base) * wx, step, 0)

    def put(m, x, i, values):
        for j in range(3):
            cst[m, re(i, j), x] = values[j][0]
            cst[m, re(i, j) + 1, x] = values[j][1]

    def site(m, n, x):
        n_own, m_ahead, n_ahead = link(own, n, x), link(plus, m, n, x), link(plus, n, m, x)
        n_back, m_back, n_diag = link(minus, n, n, x), link(minus, m, n, x), link(diag, n, m, x)
        total = link(cst, m, x)
        for i in range(3):
            part = row_times(row_of(n_own, i), m_ahead)
            acc = row_times(part, n_ahead, adj=True, acc=row_of(total, i))
            part = row_times(adj_row(n_back, i), m_back)
            put(m, x, i, row_times(part, n_diag, acc=acc))

    build_links(2)
    planes(2, site)
    for k in (2, 3, 8, 9):
        first[k].wait()
    fix_y()
    build_links(1)
    planes(1, site)
    for k in (0, 1, 4, 5, 6, 7):
        first[k].wait()
    fix_x()
    build_links(0)
    planes(0, site)

    def algebra(m, x, _):
        u, raw, target = link(own, m, x), link(cst, m, x), link(sig, m, x)
        staple = full(lambda i, j: tuple(smear_weight * v for v in raw(i, j)))
        omega = of_rows([row_times(row_of(staple, i), u, adj=True) for i in range(3)])
        a = traceless_anti(omega)
        a2 = of_rows([row_times(row_of(a, i), a) for i in range(3)])
        p = 0.5 * (a2(0, 0)[0] + a2(1, 1)[0] + a2(2, 2)[0])
        det = None
        for i in range(3):
            for j in range(3):
                v = cmul(a2(i, j), a(j, i))[1]
                det = v if det is None else det + v
        det = det * (1.0 / 3.0)
        f0 = (1.0 - det * det * (1.0 / 720), det * (1.0 / 6 + p * (1.0 / 120)))
        f1 = (1.0 + p * (1.0 / 6 + p * (1.0 / 120)), det * (1.0 / 24 + p * (1.0 / 360)))
        f2 = (0.5 + p * (1.0 / 24 + p * (1.0 / 720)), det * (1.0 / 120))
        e = []
        for i in range(3):
            e.append([])
            for j in range(3):
                v = cadd(cmul(f1, a(i, j)), cmul(f2, a2(i, j)))
                e[i].append(cadd(v, f0) if i == j else v)
        e = of_rows(e)
        direct = [row_times(adj_row(e, i), target) for i in range(3)]
        cot = of_rows([row_times(row_of(target, i), u, adj=True) for i in range(3)])
        t0 = (cot(0, 0)[0] + cot(1, 1)[0] + cot(2, 2)[0], -(cot(0, 0)[1] + cot(1, 1)[1] + cot(2, 2)[1]))
        t1, t2 = None, None
        for i in range(3):
            for j in range(3):
                g = conj(cot(i, j))
                v1, v2 = cmul(g, a(i, j)), cmul(g, a2(i, j))
                t1 = v1 if t1 is None else cadd(t1, v1)
                t2 = v2 if t2 is None else cadd(t2, v2)
        p_bar = (-t0[1] * det * (1.0 / 120) + t1[0] * (1.0 / 6 + p * (1.0 / 60))
                 - t1[1] * det * (1.0 / 360) + t2[0] * (1.0 / 24 + p * (1.0 / 360)))
        d_bar = (-t0[0] * det * (1.0 / 360) - t0[1] * (1.0 / 6 + p * (1.0 / 120))
                 - t1[1] * (1.0 / 24 + p * (1.0 / 360)) - t2[1] * (1.0 / 120))
        both = []
        for i in range(3):
            v = row_times(row_of(a, i), cot)
            both.append(row_times(row_of(cot, i), a, acc=v))
        bar = []
        g1, g2 = conj(f1), conj(f2)
        for i in range(3):
            bar.append([])
            for j in range(3):
                v1, v2 = cmul(g1, cot(i, j)), cmul(g2, both[i][j])
                aa, aq = a(i, j), a2(i, j)
                bar[i].append((v1[0] - v2[0] - p_bar * aa[0] - d_bar * aq[1],
                               v1[1] - v2[1] - p_bar * aa[1] + d_bar * aq[0]))
        alg = traceless_anti(of_rows(bar))
        for k, v in enumerate(alg_values(alg)):
            lam[m, k, x] = v
        less = [row_times(row_of(alg, i), staple) for i in range(3)]
        for i in range(3):
            for j in range(3):
                cst[m, re(i, j), x] = direct[i][j][0] - less[i][j][0]
                cst[m, re(i, j) + 1, x] = direct[i][j][1] - less[i][j][1]
        return 0

    second_x, second_y = [], []
    for m in range(4):
        lax.fori_loop(0, wx, partial(algebra, m), 0)
        slot = YSLOT[m]
        for k in range(ALG):
            for x in range(wx):
                v = lam[m, k, x]
                lyup[slot, k, x * ts:(x + 1) * ts, :] = v[(wy - 1) * ts:, :]
                if m != AXY:
                    lydn[slot, k, x * ts:(x + 1) * ts, :] = v[:ts, :]
            if m == AXX:
                lcxs[k] = lam[m, k, wx - 1][:ts, :]
            if m == AXY:
                lcys[k] = lam[m, k, 0][(wy - 1) * ts:, :]
        items = [(lam.at[m, :, wx - 1], lxm.at[m], peers[0])]
        if m != AXX:
            items.append((lam.at[m, :, 0], lxp.at[m], peers[1]))
        if m == AXX:
            items.append((lcxs, lcxy, peers[4]))
        if m == AXY:
            items.append((lcys, lcyx, peers[5]))
        second_x += exchange(items, len(first) + len(second_x) + len(second_y))
        items = [(lyup.at[slot], lym.at[slot], peers[2])]
        if m != AXY:
            items.append((lydn.at[slot], lyp.at[slot], peers[3]))
        second_y += exchange(items, len(first) + len(second_x) + len(second_y))

    def widen(load_alg, load_link, store):
        alg = alg_matrix(lambda k: smear_weight * load_alg(k))
        u = getter(load_link)
        for i in range(3):
            v = row_times(row_of(alg, i), u)
            for j in range(3):
                store(re(i, j), v[j][0])
                store(re(i, j) + 1, v[j][1])

    def widen_own(q, _):
        m, x = q // wx, lax.rem(q, wx)

        def store(c, v):
            gown[m, c, x] = v
        widen(lambda k: lam[m, k, x], lambda c: own[m, c, x], store)
        return 0

    lax.fori_loop(0, 4 * wx, widen_own, 0)
    def widen_halo(alg, ref, dst, *index):
        def store(c, v):
            dst[(*index, c)] = v
        widen(lambda k: alg[(*index, k)], lambda c: ref[(*index, c)], store)

    def widen_faces(pairs_four, pairs_three):
        def four(d, _):
            widen_halo(*pairs_four, d)
            return 0

        def three(d, _):
            widen_halo(*pairs_three, d)
            return 0

        lax.fori_loop(0, 4, four, 0)
        lax.fori_loop(1, 4, three, 0)

    def build_g(stage):
        build(gown, gplus, gminus, gdiag, gxm, gxp, gym, gyp, gcxy, gcyx, False, stage)

    def force(m, n, x):
        n_own, m_ahead, n_ahead = link(own, n, x), link(plus, m, n, x), link(plus, n, m, x)
        n_back, m_back, n_diag = link(minus, n, n, x), link(minus, m, n, x), link(diag, n, m, x)
        gn_own, gm_ahead, gn_ahead = link(gown, n, x), link(gplus, m, n, x), link(gplus, n, m, x)
        gn_back, gm_back, gn_diag = link(gminus, n, n, x), link(gminus, m, n, x), link(gdiag, n, m, x)
        total = link(cst, m, x)
        for i in range(3):
            u_row = row_of(n_own, i)
            v = row_times(u_row, gm_ahead)
            v = row_times(row_of(gn_own, i), m_ahead, acc=v)
            acc = row_times(v, n_ahead, adj=True, acc=row_of(total, i))
            v = row_times(u_row, m_ahead)
            acc = row_times(v, gn_ahead, adj=True, acc=acc)
            u_row = adj_row(n_back, i)
            v = row_times(u_row, gm_back)
            v = row_times(adj_row(gn_back, i), m_back, acc=v)
            acc = row_times(v, n_diag, acc=acc)
            v = row_times(u_row, m_back)
            put(m, x, i, row_times(v, gn_diag, acc=acc))

    build_g(2)
    planes(2, force)
    for copy in second_y:
        copy.wait()
    widen_faces((lym, hym, gym), (lyp, hyp, gyp))
    build_g(1)
    planes(1, force)
    for copy in second_x:
        copy.wait()
    widen_faces((lxm, hxm, gxm), (lxp, hxp, gxp))
    widen_halo(lcxy, cxy, gcxy)
    widen_halo(lcyx, cyx, gcyx)
    build_g(0)
    planes(0, force)

    def deliver(c, _):
        for d in range(4):
            for x in range(wx):
                for y in range(wy):
                    out[d, c, x, y] = cst[d, c, x, y * ts:(y + 1) * ts, :]
        return 0

    lax.fori_loop(0, COMP, deliver, 0)


def solution(mesh):
    sizes = (mesh.shape["gx"], mesh.shape["gy"])

    def body(links, incoming):
        dirs, _, _, _, wx, wy, _, lanes = links.shape
        ts = incoming.shape[6]
        rows = wy * ts
        flat = links.reshape(dirs, COMP, *links.shape[4:])
        flat_in = incoming.reshape(dirs, COMP, *incoming.shape[4:])
        f32 = jnp.float32

        def vm(*shape):
            return pltpu.VMEM((*shape, lanes), f32)

        field = vm(dirs, COMP, wx, rows)
        pairs = vm(dirs, dirs, COMP, wx, rows)
        halo = vm(dirs, COMP, rows)
        corner = vm(COMP, ts)
        scratch = [field, pairs, pairs, pairs, field, pairs, pairs, pairs]
        scratch += [field, field, vm(dirs, ALG, wx, rows)]
        scratch += [halo] * 4 + [corner] * 2
        scratch += [vm(SENT, ts)] * 2 + [vm(ALG, ts)] * 2
        scratch += [vm(SENT, wy)] * 2 + [vm(SENT, wx)] * 2 + [vm(COMP, wy)] * 2 + [vm(COMP, wx)] * 2
        scratch += [vm(dirs, SENT, rows)] * 2 + [vm(dirs, ALG, rows)] * 2
        scratch += [vm(dirs, ALG, rows)] * 4 + [vm(ALG, ts)] * 2
        scratch += [halo] * 4 + [corner] * 2
        scratch += [pltpu.SemaphoreType.DMA((26,)), pltpu.SemaphoreType.DMA((26,))]
        result = pl.pallas_call(
            partial(kernel, sizes),
            out_shape=jax.ShapeDtypeStruct(flat_in.shape, f32),
            in_specs=[pl.BlockSpec(memory_space=pltpu.VMEM)] * 2,
            out_specs=pl.BlockSpec(memory_space=pltpu.VMEM),
            scratch_shapes=scratch,
            compiler_params=pltpu.CompilerParams(
                collective_id=0, has_side_effects=True, vmem_limit_bytes=60 << 20),
            name="stout",
        )(flat, flat_in)
        return result.reshape(incoming.shape)

    placed = P(None, None, None, None, "gx", "gy", None, None)
    return jax.shard_map(
        body, mesh=mesh, in_specs=(placed, placed), out_specs=placed, check_vma=False)
```

profile of v0, /device:TPU:0, one launch (start us, length us, event | category | flops | bytes accessed | tf_op | source)
XLA Modules:
  0.0 41.2 jit_solution(14005395949840185426)
XLA Ops:
  0.0 2.3 %copy.3 = f32[4,3,3,2,2,2,6,128]{7,6,5,4,3,2,1,0:T(8,128)} copy(f32[4,3,3,2,2,2,6,128]{7,5,6,4,3,2,1,0:T(2,128)} %param.2) | data formatting | bytes 1769472 | tf_op args[0]
  2.4 36.9 %stout.1 = f32[4,18,2,2,4,128]{5,4,3,2,1,0:T(4,128)} custom-call(f32[4,18,2,2,6,128]{5,4,3,2,1,0:T(8,128)} %bitcast.3, f32[4,18,2,2,4,128]{5,4,3,2,1,0:T(4,128)} %bitcast.5), custom_call_target="tpu_custom_call" | custom-call | tf_op jit(solution)/shard_map/stout/pallas_call | solution.py:578
  39.3 2.0 %copy.5 = f32[4,3,3,2,2,2,4,128]{7,6,5,4,3,2,1,0:T(4,128)} copy(f32[4,3,3,2,2,2,4,128]{7,6,5,4,3,2,1,0:T(4,128)} %bitcast.4) | data formatting | bytes 1179648
where the time goes:
time: 41.5 us; the launch traced here: 41.2 us
  Pallas kernels  36.9 us (89%)
  local copies, waits for them, and re-layouts  4.3 us (10%)
    pallas_call x1, Pallas kernels, body(): pl.pallas_call(partial(kernel, sizes), out_shape=jax.ShapeDtypeStruct(fla...  36.9 us
    unnamed x2, local copies, waits for them, and re-layouts  4.3 us

commit v1 on v0

v1 whole, which is shorter than its diff:
```python
from functools import partial

import jax
import jax.numpy as jnp
from jax import lax
from jax.experimental import pallas as pl
from jax.experimental.pallas import tpu as pltpu
from jax.sharding import PartitionSpec as P

smear_weight = 0.2
MESH = pl.DeviceIdType.MESH
AXX, AXY, AXZ, AXT = 0, 1, 2, 3
SENT = 12
COMP = 18
ALG = 8
YSLOT = (1, 0, 2, 3)


def re(i, j):
    return (i * 3 + j) * 2


def conj(e):
    return (e[0], e[1], e[2], -e[3])


def dot(pairs, init=None, sign=1, parts="ri"):
    terms = {"r": [], "i": []}
    for a, b in pairs:
        for part, u, v, s in (
            ("r", 0, 0, a[2] * b[2]), ("r", 1, 1, -a[3] * b[3]),
            ("i", 0, 1, a[2] * b[3]), ("i", 1, 0, a[3] * b[2]),
        ):
            if part in parts and a[u] is not None and b[v] is not None:
                terms[part].append((sign * s, a[u], b[v]))
    out = []
    for k, part in enumerate("ri"):
        if part not in parts:
            out.append(None)
            continue
        todo = sorted(terms[part], key=lambda t: -t[0])
        total = None if init is None else init[k]
        for s, u, v in todo:
            w = u * v
            if total is None:
                total = w if s > 0 else -w
            else:
                total = total + w if s > 0 else total - w
        out.append(total)
    return tuple(out)


def elements(values):
    rows = [[(values[re(i, j)], values[re(i, j) + 1], 1, 1) for j in range(3)] for i in range(3)]
    return lambda i, j: rows[i][j]


def adjoint(mat):
    return lambda i, j: conj(mat(j, i))


def su3_product(a, b):
    rows = [[dot([(a(i, k), b(k, j)) for k in range(3)]) for j in range(3)] for i in range(2)]
    rows.append(third_row(rows))
    return [v for row in rows for e in row for v in e]


def third_row(rows):
    out = []
    for k in range(3):
        p, q = (k + 1) % 3, (k + 2) % 3
        a, b = [[(*e, 1, 1) for e in row] for row in rows]
        neg = (a[q][0], a[q][1], -1, -1)
        r, i = dot([(a[p], b[q]), (neg, b[p])], parts="r")[0], None
        i = a[q][0] * b[p][1] + a[q][1] * b[p][0] - a[p][0] * b[q][1] - a[p][1] * b[q][0]
        out.append((r, i))
    return out


def alg_elements(v):
    last = v[0] + v[1]
    diag = ((None, v[0], 1, 1), (None, v[1], 1, 1), (None, last, 1, -1))
    place = {(0, 1): 2, (0, 2): 4, (1, 2): 6}

    def get(i, j):
        if i == j:
            return diag[i]
        k = place[(min(i, j), max(i, j))]
        return (v[k], v[k + 1], 1 if i < j else -1, 1)
    return get


UPPER = ((0, 1), (0, 2), (1, 2))


def transport(g, x):
    half = [[(*dot([(g(i, k), x(k, j)) for k in range(3)]), 1, 1) for j in range(3)] for i in range(2)]
    out = [dot([(half[i][k], conj(g(i, k))) for k in range(3)], parts="i")[1] for i in range(2)]
    for i, j in UPPER:
        out += list(dot([(half[i][k], conj(g(j, k))) for k in range(3)]))
    return out


def kernel(
    sizes, links_hbm, inc_hbm, out,
    raw, inc, own, plus, prod, upper, low, lowy, tmin, tdia,
    sig, cst, lam, ahead, theta, thy,
    hxp, hyp, hly, bx0s, by0s, bx0, by0, ydn, yup,
    lxp, lyp, tyh, lydn, tyup,
    load_sem, send_sem, recv_sem,
):
    nx, ny = sizes
    wx, ts, wy, lanes = raw.shape[2], raw.shape[3] - 2, raw.shape[4], raw.shape[5]
    rows = wy * ts
    mx, my = lax.axis_index("gx"), lax.axis_index("gy")
    xu, xd = lax.rem(mx + 1, nx), lax.rem(mx + nx - 1, nx)
    yu, yd = lax.rem(my + 1, ny), lax.rem(my + ny - 1, ny)
    east, west, north, south = (xu, my), (xd, my), (mx, yu), (mx, yd)
    peers = (east, west, north, south)

    barrier = pltpu.get_barrier_semaphore()
    for peer in peers:
        pl.semaphore_signal(barrier, inc=1, device_id=peer, device_id_type=MESH)
    fetch = pltpu.make_async_copy(links_hbm, raw, load_sem.at[0])
    fetch.start()
    fetch_in = pltpu.make_async_copy(inc_hbm, inc, load_sem.at[1])
    fetch_in.start()

    row_id = lax.broadcasted_iota(jnp.int32, (rows, lanes), 0)
    y_id = lax.rem(row_id, wy)
    flat = raw.reshape(*raw.shape[:3], (ts + 2) * wy, lanes)

    def sub(v, shift):
        shift = shift % rows
        return v if shift == 0 else pltpu.roll(v, shift, 0)

    def lane(v, shift):
        return pltpu.roll(v, shift % lanes, 1)

    def pack_down(parts):
        v = parts[0]
        for x in range(1, wx):
            v = jnp.where(y_id == x, sub(parts[x], x), v)
        return v

    def pack_up(parts):
        v = sub(parts[0], 1 - wy)
        for x in range(1, wx):
            v = jnp.where(y_id == x, sub(parts[x], x + 1 - wy), v)
        return v

    def y_ahead(v, halo, x):
        return jnp.where(y_id == wy - 1, sub(halo, wy - 1 - x), sub(v, -1))

    def y_from_behind(v, halo, x):
        return jnp.where(y_id == 0, sub(halo, -x), sub(v, 1))

    def t_ahead(v):
        return jnp.where(row_id >= rows - wy, 0.0, sub(v, -wy))

    def t_behind(v):
        return jnp.where(row_id < wy, 0.0, sub(v, wy))

    def loop(n, body):
        def step(k, _):
            body(k)
            return 0
        lax.fori_loop(0, n, step, 0)

    count = [0]

    def send(src, dst, peer):
        k = count[0]
        count[0] += 1
        copy = pltpu.make_async_remote_copy(
            src_ref=src, dst_ref=dst, send_sem=send_sem.at[k],
            recv_sem=recv_sem.at[k], device_id=peer, device_id_type=MESH)
        copy.start()
        return copy

    s = pl.ds(0, SENT)
    fetch.wait()

    def compact(c):
        for d in range(4):
            for x in range(wx):
                own[d, c, x] = flat[d, c, x, wy:wy + rows, :]
    loop(COMP, compact)

    def edges(c):
        for d in (AXX, AXZ, AXT):
            ydn[YSLOT[d], c] = pack_down([own[d, c, x] for x in range(wx)])
        bx0s[c] = flat[AXT, c, 0, 0:wy, :]
        for x in range(wx):
            by0s[c, x:x + 1, :] = flat[AXT, c, x, 0:1, :]
    loop(SENT, edges)

    pl.semaphore_wait(barrier, len(peers))
    down_y = [send(ydn.at[1:4], hyp.at[1:4, s], south), send(by0s, by0.at[s], south)]
    down_x = [send(own.at[1:4, s, 0], hxp.at[1:4, s], west), send(bx0s, bx0.at[s], west)]

    def shifts(c):
        for d in range(4):
            for x in range(wx):
                tmin[d, c, x] = flat[d, c, x, 0:rows, :]
                if d != AXT:
                    plus[d, AXT, c, x] = flat[d, c, x, 2 * wy:2 * wy + rows, :]
                if d != AXZ:
                    plus[d, AXZ, c, x] = lane(own[d, c, x], -1)
        for x in range(wx):
            tdia[AXZ, c, x] = lane(tmin[AXT, c, x], -1)
    loop(COMP, shifts)

    def matrix(ref, *index):
        return elements([ref[(*index[:-1], c, index[-1])] for c in range(COMP)])

    def product(m, n, x):
        return su3_product(matrix(own, m, x), matrix(plus, n, m, x))

    def path(m, n):
        def body(x):
            p = product(m, n, x)
            for c, v in enumerate(p):
                prod[m, n, c, x] = v
            if n == AXT:
                p = su3_product(matrix(tmin, m, x), matrix(tdia, m, x))
                d = matrix(tmin, AXT, x)
            else:
                d = matrix(own, n, x)
            back = su3_product(adjoint(d), elements(p))
            for c, v in enumerate(back):
                if n == AXX:
                    low[m, n, c, x + 1] = v
                elif n == AXY:
                    lowy[m, c, x] = v
                elif n == AXZ:
                    low[m, n, c, x] = lane(v, 1)
                else:
                    low[m, n, c, x] = v
        loop(wx, body)

    def above(m, n):
        def body(x):
            r = su3_product(matrix(prod, n, m, x), adjoint(matrix(plus, n, m, x)))
            for c, v in enumerate(r):
                upper[m, n, c, x] = v
        loop(wx, body)

    def send_low_x(m):
        return send(low.at[m, AXX, s, wx], low.at[m, AXX, s, 0], east)

    def send_low_y(m):
        slot = YSLOT[m]

        def body(c):
            yup[slot, c] = pack_up([lowy[m, c, x] for x in range(wx)])
        loop(SENT, body)
        return send(yup.at[slot], hly.at[slot, s], north)

    def fix(ref, *index):
        rows_ = [[(ref[(*index, re(i, j))], ref[(*index, re(i, j) + 1)]) for j in range(3)] for i in range(2)]
        for k, e in enumerate(third_row(rows_)):
            ref[(*index, re(2, k))] = e[0]
            ref[(*index, re(2, k) + 1)] = e[1]

    up_x, up_y = [], []
    for m in (AXZ, AXT):
        path(m, AXX)
        up_x.append(send_low_x(m))
    for m in (AXZ, AXT):
        path(m, AXY)
        up_y.append(send_low_y(m))
    path(AXZ, AXT)
    path(AXT, AXZ)
    above(AXZ, AXT)
    above(AXT, AXZ)

    def convert(c):
        for d in range(4):
            for x in range(wx):
                for y in range(wy):
                    sig[d, c, x, pl.ds(y, ts, stride=wy), :] = inc[d, c, x, y]
    fetch_in.wait()
    loop(COMP, convert)

    for copy in down_y:
        copy.wait()
    loop(3, lambda d: fix(hyp, d + 1))
    fix(by0)

    def build_y(c):
        for d in (AXX, AXZ, AXT):
            for x in range(wx):
                plus[d, AXY, c, x] = y_ahead(own[d, c, x], hyp[YSLOT[d], c], x)
        for x in range(wx):
            edge = jnp.broadcast_to(by0[c, x:x + 1, :], (rows, lanes))
            v = jnp.where(row_id < wy, edge, sub(plus[AXT, AXY, c, x], wy))
            tdia[AXY, c, x] = jnp.where(row_id < wy - 1, sub(tmin[AXT, c, x], -1), v)
    loop(COMP, build_y)
    path(AXY, AXX)
    up_x.append(send_low_x(AXY))
    path(AXY, AXZ)
    path(AXY, AXT)
    for m in (AXZ, AXT):
        above(AXY, m)
        above(m, AXY)

    for copy in down_x:
        copy.wait()
    loop(3, lambda d: fix(hxp, d + 1))
    fix(bx0)

    def build_x(c):
        for d in (AXY, AXZ, AXT):
            for x in range(wx):
                plus[d, AXX, c, x] = own[d, c, x + 1] if x + 1 < wx else hxp[d, c]
        for x in range(wx - 1):
            tdia[AXX, c, x] = tmin[AXT, c, x + 1]
        edge = jnp.concatenate([bx0[c]] * ts, axis=0)
        tdia[AXX, c, wx - 1] = jnp.where(row_id < wy, edge, sub(hxp[AXT, c], wy))
    loop(COMP, build_x)
    path(AXX, AXY)
    up_y.append(send_low_y(AXX))
    path(AXX, AXZ)
    path(AXX, AXT)
    for m in (AXY, AXZ, AXT):
        above(AXX, m)
        above(m, AXX)

    def fix_low(m):
        first = [[(low[m, AXX, re(i, j), 0], low[m, AXX, re(i, j) + 1, 0]) for j in range(3)] for i in range(2)]
        for k, e in enumerate(third_row(first)):
            low[m, AXX, re(2, k), 0] = e[0]
            low[m, AXX, re(2, k) + 1, 0] = e[1]

    def finish_y(m):
        slot = YSLOT[m]
        fix(hly, slot)

        def body(c):
            for x in range(wx):
                low[m, AXY, c, x] = y_from_behind(lowy[m, c, x], hly[slot, c], x)
        loop(COMP, body)

    def algebra(m, x):
        u, target = matrix(own, m, x), matrix(sig, m, x)
        others = [n for n in range(4) if n != m]
        total = []
        for c in range(COMP):
            v = None
            for n in others:
                w = upper[m, n, c, x] + low[m, n, c, x]
                v = w if v is None else v + w
            total.append(smear_weight * v)
        staple = elements(total)

        def times_udag(left, i, j, parts="ri"):
            return dot([(left(i, k), conj(u(j, k))) for k in range(3)], parts=parts)

        diag = [times_udag(staple, i, i, "i")[1] for i in range(3)]
        third = (diag[0] + diag[1] + diag[2]) * (1.0 / 3.0)
        av = [diag[0] - third, diag[1] - third]
        for i, j in UPPER:
            p1, p2 = times_udag(staple, i, j), times_udag(staple, j, i)
            av += [0.5 * (p1[0] - p2[0]), 0.5 * (p1[1] + p2[1])]
        a = alg_elements(av)
        sq = {}
        for i in range(3):
            sq[(i, i)] = (dot([(a(i, k), a(k, i)) for k in range(3)], parts="r")[0], None, 1, 1)
        for i, j in UPPER:
            sq[(i, j)] = (*dot([(a(i, k), a(k, j)) for k in range(3)]), 1, 1)
            sq[(j, i)] = conj(sq[(i, j)])
        p = 0.5 * (sq[(0, 0)][0] + sq[(1, 1)][0] + sq[(2, 2)][0])
        every = [(i, j) for i in range(3) for j in range(3)]
        det = dot([(sq[(i, j)], a(j, i)) for i, j in every], parts="i")[1] * (1.0 / 3.0)
        f0 = (1.0 - det * det * (1.0 / 720), det * (1.0 / 6 + p * (1.0 / 120)))
        f1 = (1.0 + p * (1.0 / 6 + p * (1.0 / 120)), det * (1.0 / 24 + p * (1.0 / 360)), 1, 1)
        f2 = (0.5 + p * (1.0 / 24 + p * (1.0 / 720)), det * (1.0 / 120), 1, 1)
        e = {}
        for i, j in every:
            init = f0 if i == j else None
            e[(i, j)] = (*dot([(f1, a(i, j)), (f2, sq[(i, j)])], init=init), 1, 1)
        for i, j in every:
            v = dot([(conj(e[(k, i)]), target(k, j)) for k in range(3)])
            cst[m, re(i, j), x] = v[0]
            cst[m, re(i, j) + 1, x] = v[1]
        cot = {}
        for i, j in every:
            cot[(i, j)] = (*times_udag(target, i, j), 1, 1)
        t0 = (cot[(0, 0)][0] + cot[(1, 1)][0] + cot[(2, 2)][0],
              -(cot[(0, 0)][1] + cot[(1, 1)][1] + cot[(2, 2)][1]))
        t1 = dot([(conj(cot[ij]), a(*ij)) for ij in every])
        t2 = dot([(conj(cot[ij]), sq[ij]) for ij in every])
        p_bar = (-t0[1] * det * (1.0 / 120) + t1[0] * (1.0 / 6 + p * (1.0 / 60))
                 - t1[1] * det * (1.0 / 360) + t2[0] * (1.0 / 24 + p * (1.0 / 360)))
        d_bar = (-t0[0] * det * (1.0 / 360) - t0[1] * (1.0 / 6 + p * (1.0 / 120))
                 - t1[1] * (1.0 / 24 + p * (1.0 / 360)) - t2[1] * (1.0 / 120))
        g1, g2 = conj(f1), conj(f2)
        herm = {}
        for i in range(3):
            herm[(i, i)] = (dot([(g2, cot[(i, i)])], parts="r")[0], None, 1, 1)
        for i, j in UPPER:
            k1, k2 = dot([(g2, cot[(i, j)])]), dot([(g2, cot[(j, i)])])
            herm[(i, j)] = (0.5 * (k1[0] + k2[0]), 0.5 * (k1[1] - k2[1]), 1, 1)
            herm[(j, i)] = conj(herm[(i, j)])

        def both(i, j, parts="ri"):
            return dot([(a(i, k), herm[(k, j)]) for k in range(3)], parts=parts)

        diag = []
        for i in range(3):
            v = dot([(g1, cot[(i, i)])], parts="i")[1] - 2.0 * both(i, i, "i")[1]
            ai = a(i, i)
            w = p_bar * ai[1]
            v = v - w if ai[3] > 0 else v + w
            diag.append(v + d_bar * sq[(i, i)][0])
        third = (diag[0] + diag[1] + diag[2]) * (1.0 / 3.0)
        lv = [diag[0] - third, diag[1] - third]
        for i, j in UPPER:
            j1, j2 = dot([(g1, cot[(i, j)])]), dot([(g1, cot[(j, i)])])
            x1, x2 = both(i, j), both(j, i)
            aa, aq = a(i, j), sq[(i, j)]
            lv.append(0.5 * (j1[0] - j2[0]) - (x1[0] - x2[0]) - p_bar * aa[0] - d_bar * aq[1])
            lv.append(0.5 * (j1[1] + j2[1]) - (x1[1] + x2[1]) - p_bar * aa[1] + d_bar * aq[0])
        for k, v in enumerate(lv):
            lam[m, k, x] = smear_weight * v

    def send_lam(m):
        copies_x, copies_y = [], []
        if m != AXX:
            copies_x.append(send(lam.at[m, :, 0], lxp.at[m], west))
        if m != AXY:
            slot = YSLOT[m]
            for k in range(ALG):
                lydn[slot, k] = pack_down([lam[m, k, x] for x in range(wx)])
            copies_y.append(send(lydn.at[slot], lyp.at[slot], south))
        return copies_x, copies_y

    lam_x, lam_y = [], []
    for k, m in enumerate((AXZ, AXT, AXY, AXX)):
        if m != AXX:
            up_x[k].wait()
            fix_low(m)
        if m != AXY:
            up_y[min(k, 2)].wait()
            finish_y(m)
        loop(wx, partial(algebra, m))
        cx, cy = send_lam(m)
        lam_x += cx
        lam_y += cy

    def algebra_of(ref, *index):
        return [ref[(*index[:-1], k, index[-1])] for k in range(ALG)]

    def turn(n, m):
        def body(x):
            far = alg_elements(algebra_of(ahead, m, n, x))
            near_n, near_m = algebra_of(lam, n, x), algebra_of(lam, m, x)
            un = matrix(own, n, x)
            xs = [v + (b - c) for v, b, c in zip(transport(un, far), near_n, near_m)]
            xe = alg_elements(xs)
            for k, v in enumerate(transport(adjoint(matrix(own, m, x)), xe)):
                if m == AXX:
                    theta[n, m, k, x + 1] = v
                elif m == AXY:
                    thy[n, k, x] = v
                elif m == AXZ:
                    theta[n, m, k, x] = lane(v, 1)
                else:
                    theta[n, m, k, x] = t_behind(v)
            r = matrix(upper, m, n, x)
            for i in range(3):
                for j in range(3):
                    c = re(i, j)
                    v = dot([(xe(i, k), r(k, j)) for k in range(3)], init=(cst[m, c, x], cst[m, c + 1, x]))
                    cst[m, c, x] = v[0]
                    cst[m, c + 1, x] = v[1]
            r = matrix(upper, n, m, x)
            for i in range(3):
                for j in range(3):
                    c = re(i, j)
                    v = dot([(r(i, k), far(k, j)) for k in range(3)], init=(cst[n, c, x], cst[n, c + 1, x]), sign=-1)
                    cst[n, c, x] = v[0]
                    cst[n, c + 1, x] = v[1]
        loop(wx, body)

    def below(m, n):
        def body(x):
            xs = [b - c for b, c in zip(algebra_of(theta, m, n, x), algebra_of(lam, m, x))]
            xe, r = alg_elements(xs), matrix(low, m, n, x)
            for i in range(3):
                for j in range(3):
                    c = re(i, j)
                    v = dot([(xe(i, k), r(k, j)) for k in range(3)], init=(cst[m, c, x], cst[m, c + 1, x]))
                    cst[m, c, x] = v[0]
                    cst[m, c + 1, x] = v[1]
        loop(wx, body)

    def send_theta_x(n):
        return send(theta.at[n, AXX, :, wx], theta.at[n, AXX, :, 0], east)

    def send_theta_y(n):
        slot = YSLOT[n]
        for k in range(ALG):
            tyup[slot, k] = pack_up([thy[n, k, x] for x in range(wx)])
        return send(tyup.at[slot], tyh.at[slot], north)

    def look_zt(k):
        for m in range(4):
            for x in range(wx):
                if m != AXZ:
                    ahead[m, AXZ, k, x] = lane(lam[m, k, x], -1)
                if m != AXT:
                    ahead[m, AXT, k, x] = t_ahead(lam[m, k, x])
    loop(ALG, look_zt)
    th_x, th_y = [], []
    for n in (AXZ, AXT):
        turn(n, AXX)
        th_x.append(send_theta_x(n))
    for n in (AXZ, AXT):
        turn(n, AXY)
        th_y.append(send_theta_y(n))
    turn(AXZ, AXT)
    turn(AXT, AXZ)

    for copy in lam_y:
        copy.wait()

    def look_y(k):
        for m in (AXX, AXZ, AXT):
            for x in range(wx):
                ahead[m, AXY, k, x] = y_ahead(lam[m, k, x], lyp[YSLOT[m], k], x)
    loop(ALG, look_y)
    turn(AXY, AXX)
    th_x.append(send_theta_x(AXY))
    turn(AXY, AXZ)
    turn(AXY, AXT)

    for copy in lam_x:
        copy.wait()

    def look_x(k):
        for m in (AXY, AXZ, AXT):
            for x in range(wx):
                ahead[m, AXX, k, x] = lam[m, k, x + 1] if x + 1 < wx else lxp[m, k]
    loop(ALG, look_x)
    turn(AXX, AXY)
    th_y.append(send_theta_y(AXX))
    turn(AXX, AXZ)
    turn(AXX, AXT)

    for m in range(4):
        for n in (AXZ, AXT):
            if m != n:
                below(m, n)
    for k, m in enumerate((AXZ, AXT, AXY)):
        th_x[k].wait()
        below(m, AXX)
    for k, m in enumerate((AXZ, AXT, AXX)):
        th_y[k].wait()

        def meet(k, m=m):
            for x in range(wx):
                theta[m, AXY, k, x] = y_from_behind(thy[m, k, x], tyh[YSLOT[m], k], x)
        loop(ALG, meet)
        below(m, AXY)

    def deliver(c):
        for d in range(4):
            for x in range(wx):
                for y in range(wy):
                    out[d, c, x, y * ts:(y + 1) * ts, :] = cst[d, c, x, pl.ds(y, ts, stride=wy), :]
    loop(COMP, deliver)


def solution(mesh):
    sizes = (mesh.shape["gx"], mesh.shape["gy"])

    def body(links, incoming):
        dirs, _, _, _, wx, wy, _, lanes = links.shape
        ts = incoming.shape[6]
        rows = wy * ts
        assert wx <= wy
        turned = links.transpose(0, 1, 2, 3, 4, 6, 5, 7)
        flat = turned.reshape(dirs, COMP, wx, ts + 2, wy, lanes)
        flat_in = incoming.reshape(dirs, COMP, *incoming.shape[4:])
        f32 = jnp.float32

        def vm(*shape):
            return pltpu.VMEM((*shape, lanes), f32)

        field = vm(dirs, COMP, wx, rows)
        pairs = vm(dirs, dirs, COMP, wx, rows)
        halo = vm(dirs, COMP, rows)
        scratch = [pltpu.VMEM(flat.shape, f32), pltpu.VMEM(flat_in.shape, f32)]
        scratch += [field, pairs, pairs, pairs, vm(dirs, dirs, COMP, wx + 1, rows), field, field, field]
        scratch += [field, field, vm(dirs, ALG, wx, rows), vm(dirs, dirs, ALG, wx, rows)]
        scratch += [vm(dirs, dirs, ALG, wx + 1, rows), vm(dirs, ALG, wx, rows)]
        scratch += [halo] * 3 + [vm(SENT, wy), vm(SENT, wx), vm(COMP, wy), vm(COMP, wx)]
        scratch += [vm(dirs, SENT, rows)] * 2 + [vm(dirs, ALG, rows)] * 5
        scratch += [pltpu.SemaphoreType.DMA((2,))] + [pltpu.SemaphoreType.DMA((22,))] * 2
        result = pl.pallas_call(
            partial(kernel, sizes),
            out_shape=jax.ShapeDtypeStruct((dirs, COMP, wx, rows, lanes), f32),
            in_specs=[pl.BlockSpec(memory_space=pl.ANY)] * 2,
            out_specs=pl.BlockSpec(memory_space=pltpu.VMEM),
            scratch_shapes=scratch,
            compiler_params=pltpu.CompilerParams(
                collective_id=0, has_side_effects=True, vmem_limit_bytes=60 << 20),
            name="stout",
        )(flat, flat_in)
        return result.reshape(incoming.shape)

    placed = P(None, None, None, None, "gx", "gy", None, None)
    return jax.shard_map(
        body, mesh=mesh, in_specs=(placed, placed), out_specs=placed, check_vma=False)
```

time: 41.5 us -> 27.4 us (0.66)
  Pallas kernels: 36.9 us -> 25.2 us
  local copies, waits for them, and re-layouts: 4.3 us -> 1.95 us
    pallas_call x1, Pallas kernels: 36.9 us -> 25.2 us  [body(): pl.pallas_call(partial(kernel, sizes), out_shape=jax.ShapeDtypeStruct((di...]
    unnamed x2 -> x1, local copies, waits for them, and re-layouts: 4.3 us -> 1.95 us
where the time goes in v1:
time: 27.4 us; the launch traced here: 27.2 us
  Pallas kernels  25.2 us (92%)
  local copies, waits for them, and re-layouts  1.95 us (7%)
    pallas_call x1, Pallas kernels, body(): pl.pallas_call(partial(kernel, sizes), out_shape=jax.ShapeDtypeStruct((di...  25.2 us
    unnamed x1, local copies, waits for them, and re-layouts  1.95 us

profile of v1, /device:TPU:0, one launch (start us, length us, event | category | flops | bytes accessed | tf_op | source)
XLA Modules:
  0.0 27.2 jit_solution(11928331200474054120)
XLA Ops:
  0.0 25.2 %stout.1 = f32[4,18,2,8,128]{4,3,2,1,0:T(8,128)} custom-call(f32[4,18,2,6,2,128]{5,4,3,2,1,0:T(2,128)} %bitcast.6, f32[4,18,2,2,4,128]{5,4,3,2,1,0:T(4,128)} %bitcast.7), custom_call_target="tpu_custom_call" | custom-call | tf_op jit(solution)/shard_map/stout/pallas_call | solution.py:602
  25.2 2.0 %copy.4 = f32[4,3,3,2,2,2,4,128]{7,6,5,4,3,2,1,0:T(4,128)} copy(f32[4,3,3,2,2,2,4,128]{7,6,5,4,3,2,1,0:T(4,128)} %bitcast.5) | data formatting | bytes 1179648
